TPU v7x, 256 devices: a whole 4x4x8 slice. The times are simulated.
256 devices in a mesh: ctx: 32 (over x, z), tp: 8 (over y, core).
Axes of the slice: x: 4, y: 4, z: 8, core: 2. Of those that a mesh axis runs over, the one named last changes fastest.
Arguments:
- hidden_in: bfloat16 [8192, 3072], P('ctx', 'tp'), may hold values from -96 to 96
- norm_gain: float32 [3072], replicated, may hold values from 0.1 to 1.9
- w_query: bfloat16 [3072, 3072], P(None, 'tp'), may hold values from -1 to 1
- w_key: bfloat16 [3072, 3072], P(None, 'tp'), may hold values from -1 to 1
- w_value: bfloat16 [3072, 3072], P(None, 'tp'), may hold values from -0.109375 to 0.109375
- w_out: bfloat16 [3072, 3072], P('tp'), may hold values from -0.109375 to 0.109375
- head_gain: float32 [3072], replicated, may hold values from 0.1 to 1.9
- proj_head: bfloat16 [3072, 2048], P('tp'), may hold values from -0.109375 to 0.109375
- proj_middle: bfloat16 [3072, 512], P('tp'), may hold values from -0.109375 to 0.109375
- proj_tail: bfloat16 [3072, 128], P('tp'), may hold values from -0.109375 to 0.109375
- table_head: bfloat16 [10240, 2048], P(('tp', 'ctx')), may hold values from -64 to 64
- table_middle: bfloat16 [20480, 512], P(('tp', 'ctx')), may hold values from -64 to 64
- table_tail: bfloat16 [104448, 128], P(('tp', 'ctx')), may hold values from -64 to 64
- clusters: bfloat16 [2, 2048], replicated, may hold values from -0.375 to 0.375
- targets: int32 [8192], P('ctx'), may hold values from 0 to 135167
Outputs:
- hidden_out: bfloat16 [8192, 3072], P('ctx', 'tp')
- losses: float32 [8192], P('ctx')
All inputs are finite; a program needn't handle non-finite values.
Results may differ from a plain program's by a relative error of at most 0.004.
Values may be sent and summed in bfloat16 or wider, within the bound.
No kernel may reach another device: no remote copies, remote signals or barrier semaphores. Data moves between devices by JAX's collectives and lax.ppermute only.
A program may use at most 128 MiB of HBM per device.

v0:
```python
import jax
import jax.numpy as jnp
from jax import lax
from jax.sharding import PartitionSpec as P

D = 3072
HD = 96
V0 = 10240
V1 = 20480
NEG_FILL = -1e30


def passed_along(block, axis, distance):
    devices = range(lax.axis_size(axis))
    route = [(i - distance, i) for i in devices if i - distance in devices]
    return lax.ppermute(block, axis, route)


def merged(part, axis, combine):
    gathered = jax.tree.map(lambda a: lax.all_gather(a, axis), part)

    def take(source):
        return jax.tree.map(lambda a: lax.dynamic_index_in_dim(a, source, 0, False), gathered)

    return lax.fori_loop(
        1, lax.axis_size(axis), lambda source, state: combine(state, take(source)), take(0)
    )


def merge_stats(first_stats, second_stats):
    top_value = jnp.maximum(first_stats[0], second_stats[0])
    sum_exp = first_stats[1] * jnp.exp(first_stats[0] - top_value) + second_stats[1] * jnp.exp(
        second_stats[0] - top_value
    )
    return (top_value, sum_exp, first_stats[2] + second_stats[2])


def merge_bands(first_bands, second_bands):
    return tuple(
        (
            merge_stats(one_band, other_band)
            for one_band, other_band in zip(first_bands, second_bands)
        )
    )


def empty_stats(row_total):
    return (
        jnp.full((row_total,), NEG_FILL, jnp.float32),
        jnp.zeros((row_total,), jnp.float32),
        jnp.zeros((row_total,), jnp.float32),
    )


def fold_band(running, table_part, band_rows, local_goal):
    row_count = table_part.shape[0]
    block_rows = min(row_count, 2048)
    for row_start in range(0, row_count, block_rows):
        table_slab = table_part[row_start : row_start + block_rows]
        logits = lax.dot_general(
            table_slab, band_rows, (((1,), (1,)), ((), ())), preferred_element_type=jnp.float32
        )
        word_index = lax.broadcasted_iota(jnp.int32, logits.shape, 0) + row_start
        block_top = jnp.max(logits, 0)
        block_sum = jnp.sum(jnp.exp(logits - block_top[None]), 0)
        block_pick = jnp.sum(jnp.where(word_index == local_goal[None], logits, 0.0), 0)
        running = merge_stats(running, (block_top, block_sum, block_pick))
    return running


def scale_rows(row_values, square_sums, gain_part):
    return (row_values * lax.rsqrt(square_sums / D + 1e-06)[:, None] * gain_part).astype(
        jnp.bfloat16
    )


def project(full_rows, weight):
    return jnp.dot(full_rows, weight, preferred_element_type=jnp.float32).astype(jnp.bfloat16)


def body(
    hidden_in,
    norm_gain,
    w_query,
    w_key,
    w_value,
    w_out,
    head_gain,
    proj_head,
    proj_middle,
    proj_tail,
    table_head,
    table_middle,
    table_tail,
    clusters,
    targets,
):
    seg_len = hidden_in.shape[0]
    local_width = hidden_in.shape[1]
    tp_rank = lax.axis_index("tp")
    ctx_rank = lax.axis_index("ctx")
    ctx_count = lax.axis_size("ctx")
    gain_in = lax.dynamic_slice_in_dim(norm_gain, tp_rank * local_width, local_width)
    gain_out = lax.dynamic_slice_in_dim(head_gain, tp_rank * local_width, local_width)
    own_rows = hidden_in.astype(jnp.float32)
    own_sq = lax.psum(jnp.sum(own_rows * own_rows, 1), "tp")
    own_full = lax.all_gather(scale_rows(own_rows, own_sq, gain_in), "tp", axis=1, tiled=True)
    queries = project(own_full, w_query)
    keys_now = project(own_full, w_key)
    values_now = project(own_full, w_value)
    key_width = keys_now.shape[1]
    carried = passed_along(jnp.concatenate([keys_now, values_now], 1), "ctx", 1)
    memory_keys = carried[:, :key_width]
    memory_values = carried[:, key_width:]
    heads_local = queries.shape[1] // HD
    query_heads = queries.reshape(seg_len, heads_local, HD)
    key_heads = jnp.concatenate([memory_keys, keys_now], 0).reshape(2 * seg_len, heads_local, HD)
    value_heads = jnp.concatenate([memory_values, values_now], 0).reshape(
        2 * seg_len, heads_local, HD
    )
    scores = jnp.einsum(
        "qhe,khe->hqk", query_heads, key_heads, preferred_element_type=jnp.float32
    ) * HD ** (-0.5)
    row_pos = lax.broadcasted_iota(jnp.int32, (seg_len, 2 * seg_len), 0)
    col_pos = lax.broadcasted_iota(jnp.int32, (seg_len, 2 * seg_len), 1)
    allowed = jnp.where(col_pos < seg_len, ctx_rank > 0, col_pos - seg_len <= row_pos)
    scores = jnp.where(allowed[None], scores, NEG_FILL)
    top_score = jnp.max(scores, axis=2, keepdims=True)
    raised = jnp.exp(scores - top_score)
    weights = (raised / jnp.sum(raised, axis=2, keepdims=True)).astype(jnp.bfloat16)
    context = jnp.einsum("hqk,khe->qhe", weights, value_heads, preferred_element_type=jnp.float32)
    context = context.astype(jnp.bfloat16).reshape(seg_len, heads_local * HD)
    partial_out = jnp.dot(context, w_out, preferred_element_type=jnp.float32)
    attention = lax.psum_scatter(
        partial_out.astype(jnp.bfloat16), "tp", scatter_dimension=1, tiled=True
    ).astype(jnp.float32)
    summed = own_rows + attention
    hidden_out = summed.astype(jnp.bfloat16)
    out_sq = lax.psum(jnp.sum(summed * summed, 1), "tp")
    normed_out = scale_rows(summed, out_sq, gain_out)
    band_sums = (
        lax.psum(
            jnp.dot(normed_out, proj_head, preferred_element_type=jnp.float32).astype(jnp.bfloat16),
            "tp",
        ).astype(jnp.float32),
        lax.psum(
            jnp.dot(normed_out, proj_middle, preferred_element_type=jnp.float32).astype(
                jnp.bfloat16
            ),
            "tp",
        ).astype(jnp.float32),
        lax.psum(
            jnp.dot(normed_out, proj_tail, preferred_element_type=jnp.float32).astype(jnp.bfloat16),
            "tp",
        ).astype(jnp.float32),
    )
    inputs_head = band_sums[0].astype(jnp.bfloat16)
    inputs_middle = band_sums[1].astype(jnp.bfloat16)
    inputs_tail = band_sums[2].astype(jnp.bfloat16)
    rows_head = table_head.shape[0]
    rows_middle = table_middle.shape[0]
    rows_tail = table_tail.shape[0]
    head_base = tp_rank * rows_head * ctx_count
    head_stats = fold_band(
        empty_stats(seg_len),
        lax.all_gather(table_head, "ctx", axis=0, tiled=True),
        inputs_head,
        targets - head_base,
    )
    middle_base = tp_rank * rows_middle * ctx_count
    tail_base = tp_rank * rows_tail * ctx_count
    middle_stats = fold_band(
        empty_stats(seg_len),
        lax.all_gather(table_middle, "ctx", axis=0, tiled=True),
        inputs_middle,
        targets - V0 - middle_base,
    )
    tail_stats = fold_band(
        empty_stats(seg_len),
        lax.all_gather(table_tail, "ctx", axis=0, tiled=True),
        inputs_tail,
        targets - V0 - V1 - tail_base,
    )
    head_stats, middle_stats, tail_stats = merged(
        (head_stats, middle_stats, tail_stats), "tp", merge_bands
    )
    word_total = head_stats[0] + jnp.log(head_stats[1])
    cluster_logits = lax.dot_general(
        inputs_head, clusters, (((1,), (1,)), ((), ())), preferred_element_type=jnp.float32
    )
    first_cluster = cluster_logits[:, 0]
    second_cluster = cluster_logits[:, 1]
    highest = jnp.maximum(word_total, jnp.maximum(first_cluster, second_cluster))
    head_total = highest + jnp.log(
        jnp.exp(word_total - highest)
        + jnp.exp(first_cluster - highest)
        + jnp.exp(second_cluster - highest)
    )
    middle_total = middle_stats[0] + jnp.log(middle_stats[1])
    tail_total = tail_stats[0] + jnp.log(tail_stats[1])
    loss_head = head_total - head_stats[2]
    loss_middle = head_total - first_cluster + middle_total - middle_stats[2]
    loss_tail = head_total - second_cluster + tail_total - tail_stats[2]
    losses = jnp.where(
        targets < V0, loss_head, jnp.where(targets < V0 + V1, loss_middle, loss_tail)
    )
    return (hidden_out, losses)


def solution(mesh):
    placed = (
        P("ctx", "tp"),
        P(),
        P(None, "tp"),
        P(None, "tp"),
        P(None, "tp"),
        P("tp", None),
        P(),
        P("tp", None),
        P("tp", None),
        P("tp", None),
        P(("tp", "ctx"), None),
        P(("tp", "ctx"), None),
        P(("tp", "ctx"), None),
        P(),
        P("ctx"),
    )
    return jax.shard_map(
        body, mesh=mesh, in_specs=placed, out_specs=(P("ctx", "tp"), P("ctx")), check_vma=False
    )
```

profile of v0, /device:TPU:1, one launch (start us, length us, event | category | flops | bytes accessed | tf_op | source)
XLA Modules:
  0.0 371.5 jit_solution(5474773820088857261)
XLA Ops:
  8.1 1.2 fusion.52
  9.3 15.0 %psum.35 = f32[256]{0:T(256)S(1)} all-reduce(f32[256]{0:T(256)S(1)} %fusion.52), channel_id=1, replica_groups=mesh['ctx'=32,'tp'=8] {'tp'}, use_global_device_ids=true, to_apply=%region_1.0 | all-reduce | flops 256 | bytes 2048 | tf_op jit(solution)/shard_map/psum | solution.py:106
  24.2 0.8 dynamic_slice.124
  25.0 1.7 fusion.54
  26.8 28.5 %all-gather.17.cloned.1.call-done = bf16[256,3072]{1,0:T(8,128)(2,1)} async-done(((bf16[256,384]{1,0:T(8,128)(2,1)}), bf16[256,3072]{1,0:T(8,128)(2,1)}) %all-gather.17.cloned.1.call-update) | async-done | bytes 1572880 | tf_op jit(solution)/shard_map/all_gather | solution.py:107
  55.4 3.3 convolution_convert_fusion.4
  58.7 1.0 convolution_convert_fusion.5
  59.7 3.3 collective-permute-start
  63.0 0.7 fusion.51
  63.7 1.7 convolution_convert_fusion.3
  65.4 1.7 copy.24
  67.1 4.0 %collective-permute-done = bf16[256,768]{1,0:T(8,128)(2,1)S(1)} collective-permute-done((bf16[256,768]{1,0:T(8,128)(2,1)S(1)}, bf16[256,768]{1,0:T(8,128)(2,1)S(1)}, u32[]{:S(2)}, u32[]{:S(2)}) %collective-permute-start) | collective-permute-done | bytes 393248 | tf_op jit(solution)/shard_map/ppermute | solution.py:16
  71.2 0.1 pad_maximum_fusion.1
  71.3 0.2 copy.23
  71.5 0.2 copy.25
  71.7 2.0 fusion.69
  73.7 2.0 convolution_convert_fusion.6
  75.8 2.2 convolution_convert_fusion
  77.9 2.6 copy.26
  80.6 0.0 all-gather.21.cloned.1.call-start
  80.6 0.5 all-gather.21.cloned.1.call-update
  81.2 0.8 dynamic_slice.125
  82.0 34.9 %reduce-scatter.4.cloned.1.call-done = bf16[384,256]{1,0:T(8,128)(2,1)} async-done(((bf16[3072,256]{1,0:T(8,128)(2,1)}), bf16[384,256]{1,0:T(8,128)(2,1)}) %reduce-scatter.4.cloned.1.call-update) | async-done | bytes 196624
  116.9 1.1 copy.27
  118.0 0.1 multiply_reduce_fusion
  118.1 14.5 %psum.36 = f32[256]{0:T(256)S(1)} all-reduce(f32[256]{0:T(256)S(1)} %multiply_reduce_fusion), channel_id=1, replica_groups=mesh['ctx'=32,'tp'=8] {'tp'}, use_global_device_ids=true, to_apply=%region_6.7 | all-reduce | flops 256 | bytes 2048 | tf_op jit(solution)/shard_map/psum | solution.py:139
  132.6 0.7 multiply_convert_fusion
  133.4 0.8 convolution_convert_fusion.7
  134.2 1.0 convolution_convert_fusion.2
  135.2 1.7 convolution_convert_fusion.1
  136.9 0.0 all-gather.23.cloned.1.call-start
  137.0 0.5 all-gather.23.cloned.1.call-update
  137.6 0.5 all-gather.19.cloned.1.call-update
  138.2 22.5 %all-gather.21.cloned.1.call-done = bf16[2560,512]{1,0:T(8,128)(2,1)} async-done(((bf16[80,512]{1,0:T(8,128)(2,1)}), bf16[2560,512]{1,0:T(8,128)(2,1)}) %all-gather.21.cloned.1.call-update) | async-done | bytes 2621456 | tf_op jit(solution)/shard_map/all_gather | solution.py:174
  160.7 43.5 %all-reduce.3.cloned.1.call-done = (bf16[256,2048]{1,0:T(8,128)(2,1)}, bf16[256,512]{1,0:T(8,128)(2,1)}, bf16[256,128]{1,0:T(8,128)(2,1)}) async-done(((bf16[256,2048]{1,0:T(8,128)(2,1)}, bf16[256,512]{1,0:T(8,128)(2,1)}, bf16[256,128]{1,0:T(8,128)(2,1)}), (bf16[256,2048]{1,0:T(8,128)(2,1)}, bf16[256,512]{1,0:T(8,128)(2,1)}, bf16[256,128]{1,0:T(8,128)(2,1)})) %all-reduce.3.cloned.1.call-update) | async-done | bytes 1376272 | tf_op jit(solution)/shard_map/psum | solution.py:142
  204.2 1.5 fusion.71
  205.8 0.3 fusion.50
  206.1 2.5 fusion.72
  208.6 0.8 fusion.23
  209.4 10.6 %all-gather.7 = f32[8,1,256]{2,1,0:T(1,128)S(1)} all-gather(f32[1,1,256]{2,1,0:T(1,128)S(1)} %get-tuple-element.552), channel_id=1, replica_groups=mesh['ctx'=32,'tp'=8] {'tp'}, dimensions={0}, use_global_device_ids=true | all-gather | bytes 9216 | tf_op jit(solution)/shard_map/all_gather | solution.py:20
  220.0 9.4 %all-gather.8 = f32[8,1,256]{2,1,0:T(1,128)S(1)} all-gather(f32[1,1,256]{2,1,0:T(1,128)S(1)} %bitcast.286), channel_id=3, replica_groups=mesh['ctx'=32,'tp'=8] {'tp'}, dimensions={0}, use_global_device_ids=true | all-gather | bytes 9216 | tf_op jit(solution)/shard_map/all_gather | solution.py:20
  229.4 8.4 %all-gather.6 = f32[8,1,256]{2,1,0:T(1,128)S(1)} all-gather(f32[1,1,256]{2,1,0:T(1,128)S(1)} %get-tuple-element.553), channel_id=1, replica_groups=mesh['ctx'=32,'tp'=8] {'tp'}, dimensions={0}, use_global_device_ids=true | all-gather | bytes 9216 | tf_op jit(solution)/shard_map/all_gather | solution.py:20
  237.8 2.7 all-gather.23.cloned.1.call-done
  240.5 1.4 fusion.73
  241.9 0.4 fusion.33
  242.3 1.6 fusion.78
  243.9 0.5 fusion.77
  244.4 0.5 fusion.76
  244.9 0.5 fusion.75
  245.4 0.5 fusion.74
  245.9 0.5 fusion.79
  246.5 3.4 fusion.17
  249.9 15.1 %all-gather.10 = f32[8,1,256]{2,1,0:T(1,128)S(1)} all-gather(f32[1,1,256]{2,1,0:T(1,128)S(1)} %get-tuple-element.548), channel_id=1, replica_groups=mesh['ctx'=32,'tp'=8] {'tp'}, dimensions={0}, use_global_device_ids=true | all-gather | bytes 9216 | tf_op jit(solution)/shard_map/all_gather | solution.py:20
  265.0 8.2 %all-gather.11 = f32[8,1,256]{2,1,0:T(1,128)S(1)} all-gather(f32[1,1,256]{2,1,0:T(1,128)S(1)} %bitcast.287), channel_id=4, replica_groups=mesh['ctx'=32,'tp'=8] {'tp'}, dimensions={0}, use_global_device_ids=true | all-gather | bytes 9216 | tf_op jit(solution)/shard_map/all_gather | solution.py:20
  273.2 9.5 %all-gather.9 = f32[8,1,256]{2,1,0:T(1,128)S(1)} all-gather(f32[1,1,256]{2,1,0:T(1,128)S(1)} %get-tuple-element.549), channel_id=1, replica_groups=mesh['ctx'=32,'tp'=8] {'tp'}, dimensions={0}, use_global_device_ids=true | all-gather | bytes 9216 | tf_op jit(solution)/shard_map/all_gather | solution.py:20
  282.7 0.4 fusion.80
  283.1 42.6 %all-gather.19.cloned.1.call-done = bf16[1280,2048]{1,0:T(8,128)(2,1)} async-done(((bf16[40,2048]{1,0:T(8,128)(2,1)}), bf16[1280,2048]{1,0:T(8,128)(2,1)}) %all-gather.19.cloned.1.call-update) | async-done | bytes 5242896 | tf_op jit(solution)/shard_map/all_gather | solution.py:166
  325.7 4.1 %fusion.70 = (f32[256]{0:T(256)S(1)}, f32[256,1280]{1,0:T(8,128)S(1)}) fusion(bf16[256,2048]{1,0:T(8,128)(2,1)S(1)} %copy-done.5, bf16[1280,2048]{1,0:T(8,128)(2,1)} %all-gather.19.cloned.1.call-done), kind=kOutput, calls=%fused_computation.154 | convolution fusion | flops 1342504704 | bytes 7603200 | tf_op jit(solution)/shard_map/dot_general | solution.py:60
  329.8 0.5 fusion.27
  330.4 14.1 %all-gather.4 = f32[8,1,256]{2,1,0:T(1,128)S(1)} all-gather(f32[1,1,256]{2,1,0:T(1,128)S(1)} %get-tuple-element.557), channel_id=1, replica_groups=mesh['ctx'=32,'tp'=8] {'tp'}, dimensions={0}, use_global_device_ids=true | all-gather | bytes 9216 | tf_op jit(solution)/shard_map/all_gather | solution.py:20
  344.5 8.1 %all-gather.5 = f32[8,1,256]{2,1,0:T(1,128)S(1)} all-gather(f32[1,1,256]{2,1,0:T(1,128)S(1)} %bitcast.281), channel_id=2, replica_groups=mesh['ctx'=32,'tp'=8] {'tp'}, dimensions={0}, use_global_device_ids=true | all-gather | bytes 9216 | tf_op jit(solution)/shard_map/all_gather | solution.py:20
  352.7 9.5 %all-gather.3 = f32[8,1,256]{2,1,0:T(1,128)S(1)} all-gather(f32[1,1,256]{2,1,0:T(1,128)S(1)} %get-tuple-element.558), channel_id=1, replica_groups=mesh['ctx'=32,'tp'=8] {'tp'}, dimensions={0}, use_global_device_ids=true | all-gather | bytes 9216 | tf_op jit(solution)/shard_map/all_gather | solution.py:20
  362.2 1.4 while.31
  363.6 0.6 compare_select_fusion.1
  (157 shorter events, 1.6 us)
Async XLA Ops:
  8.0 67.8 %copy-start = (bf16[384,3072]{1,0:T(8,128)(2,1)S(1)}, bf16[384,3072]{1,0:T(8,128)(2,1)}, u32[]{:S(2)}) copy-start(bf16[384,3072]{1,0:T(8,128)(2,1)} %param.22) | copy-start | bytes 7077892
  8.0 47.3 %all-gather.17.cloned.1.call-start = ((), (), s32[]{:S(2)}) async-start(), calls=%async_computation.1 | async-start | bytes 1769472 | tf_op jit(solution)/shard_map/all_gather | solution.py:107
  26.8 90.1 %reduce-scatter.4.cloned.1.call-start = ((), (), s32[]{:S(2)}) async-start(), calls=%async_computation.5 | async-start | bytes 1769472
  55.4 3.3 copy-start.14
  55.4 3.3 copy-start.16
  58.7 5.1 %copy-start.15 = (bf16[3072,384]{1,0:T(8,128)(2,1)S(1)}, bf16[3072,384]{1,0:T(8,128)(2,1)}, u32[]{:S(2)}) copy-start(bf16[3072,384]{1,0:T(8,128)(2,1)} %param.19) | copy-start | bytes 7077892
  59.7 11.5 %collective-permute-start = (bf16[256,768]{1,0:T(8,128)(2,1)S(1)}, bf16[256,768]{1,0:T(8,128)(2,1)S(1)}, u32[]{:S(2)}, u32[]{:S(2)}) collective-permute-start(bf16[256,768]{1,0:T(8,128)(2,1)S(1)} %pad_maximum_fusion), channel_id=1, source_target_pairs={{0,8},{8,16},{16,24},{24,32},{32,40},{40,48},{48,56},{56,64},{64,7... | collective-permute-start | bytes 1179656 | tf_op jit(solution)/shard_map/ppermute | solution.py:16
  71.7 2.0 copy-start.7
  77.9 40.0 %copy-start.3 = (bf16[256,384]{1,0:T(8,128)(2,1)S(1)}, bf16[256,384]{1,0:T(8,128)(2,1)}, u32[]{:S(2)}) copy-start(bf16[256,384]{1,0:T(8,128)(2,1)} %param.17) | copy-start | bytes 589828
  80.5 52.8 %copy-start.8 = (bf16[384,128]{1,0:T(8,128)(2,1)S(1)}, bf16[384,128]{1,0:T(8,128)(2,1)}, u32[]{:S(2)}) copy-start(bf16[384,128]{1,0:T(8,128)(2,1)} %param.26) | copy-start | bytes 294916
  80.5 53.7 %copy-start.6 = (bf16[384,512]{1,0:T(8,128)(2,1)S(1)}, bf16[384,512]{1,0:T(8,128)(2,1)}, u32[]{:S(2)}) copy-start(bf16[384,512]{1,0:T(8,128)(2,1)} %param.25) | copy-start | bytes 1179652
  80.6 80.2 %all-gather.21.cloned.1.call-start = ((), (), s32[]{:S(2)}) async-start(), calls=%async_computation.3 | async-start | bytes 2703360 | tf_op jit(solution)/shard_map/all_gather | solution.py:174
  81.2 123.1 %all-reduce.3.cloned.1.call-start = ((), (), s32[]{:S(2)}) async-start(), calls=%async_computation.6 | async-start | bytes 2752512 | tf_op jit(solution)/shard_map/psum | solution.py:142
  132.6 2.6 copy-start.4
  135.2 3.0 copy-start.13
  136.9 103.5 %all-gather.23.cloned.1.call-start = ((), (), s32[]{:S(2)}) async-start(), calls=%async_computation.4 | async-start | bytes 3446784 | tf_op jit(solution)/shard_map/all_gather | solution.py:180
  137.5 188.2 %all-gather.19.cloned.1.call-start = ((), (), s32[]{:S(2)}) async-start(), calls=%async_computation.2 | async-start | bytes 5406720 | tf_op jit(solution)/shard_map/all_gather | solution.py:166
  208.6 31.9 %copy-start.2 = (bf16[256,128]{1,0:T(8,128)(2,1)S(1)}, bf16[256,128]{1,0:T(8,128)(2,1)}, u32[]{:S(2)}) copy-start(bf16[256,128]{1,0:T(8,128)(2,1)} %get-tuple-element.529) | copy-start | bytes 196612
  220.0 23.9 %copy-start.10 = (f32[8,1,256]{2,1,0:T(1,128)}, f32[8,1,256]{2,1,0:T(1,128)S(1)}, u32[]{:S(2)}) copy-start(f32[8,1,256]{2,1,0:T(1,128)S(1)} %all-gather.7) | copy-start | bytes 24580
  229.4 14.5 %copy-start.9 = (f32[8,1,256]{2,1,0:T(1,128)}, f32[8,1,256]{2,1,0:T(1,128)S(1)}, u32[]{:S(2)}) copy-start(f32[8,1,256]{2,1,0:T(1,128)S(1)} %all-gather.8) | copy-start | bytes 24580
  237.8 6.1 %copy-start.11 = (f32[8,1,256]{2,1,0:T(1,128)}, f32[8,1,256]{2,1,0:T(1,128)S(1)}, u32[]{:S(2)}) copy-start(f32[8,1,256]{2,1,0:T(1,128)S(1)} %all-gather.6) | copy-start | bytes 24580
  240.5 3.4 copy-start.1
  246.5 36.2 %copy-start.5 = (bf16[256,2048]{1,0:T(8,128)(2,1)S(1)}, bf16[256,2048]{1,0:T(8,128)(2,1)}, u32[]{:S(2)}) copy-start(bf16[256,2048]{1,0:T(8,128)(2,1)} %get-tuple-element.527) | copy-start | bytes 3145732
  246.5 36.2 %copy-start.12 = (bf16[2,2048]{1,0:T(2,128)(2,1)S(1)}, bf16[2,2048]{1,0:T(2,128)(2,1)}, u32[]{:S(2)}) copy-start(bf16[2,2048]{1,0:T(2,128)(2,1)} %param.30) | copy-start | bytes 24580
  283.1 79.1 %slice-start = ((f32[8,1,256]{2,1,0:T(1,128)}), f32[1,1,256]{2,1,0:T(1,128)S(1)}, s32[]{:S(2)}) async-start(f32[8,1,256]{2,1,0:T(1,128)} %copy-done.9), calls=%async_computation.7 | async-start | bytes 2048 | tf_op jit(solution)/shard_map/jit(dynamic_index_in_dim)/dynamic_slice | solution.py:23
  283.1 79.1 %slice-start.1 = ((f32[8,1,256]{2,1,0:T(1,128)}), f32[1,1,256]{2,1,0:T(1,128)S(1)}, s32[]{:S(2)}) async-start(f32[8,1,256]{2,1,0:T(1,128)} %copy-done.10), calls=%async_computation.8 | async-start | bytes 2048 | tf_op jit(solution)/shard_map/jit(dynamic_index_in_dim)/dynamic_slice | solution.py:23
  283.1 79.1 %slice-start.2 = ((f32[8,1,256]{2,1,0:T(1,128)}), f32[1,1,256]{2,1,0:T(1,128)S(1)}, s32[]{:S(2)}) async-start(f32[8,1,256]{2,1,0:T(1,128)} %copy-done.11), calls=%async_computation.9 | async-start | bytes 2048 | tf_op jit(solution)/shard_map/jit(dynamic_index_in_dim)/dynamic_slice | solution.py:23
Sparse Core Ops, SparseCore 0:
  26.9 28.4 all-gather.16
  80.7 36.1 reduce-scatter.3
  137.1 67.1 all-reduce.2
Sparse Core Ops, SparseCore 1:
  83.6 77.0 all-gather.20
  163.2 77.2 all-gather.22
  242.9 82.7 all-gather.18
where the time goes:
time: 372 us
  waiting for transfers between devices  180 us (48%)
  blocking collectives  122 us (33%)
  matrix products  29.8 us (8%)
  between operations  15.8 us (4%)
  other arithmetic  11.3 us (3%)
  local copies, waits for them, and re-layouts  7.9 us (2%)
    all_gather x9, blocking collectives, merged(): gathered = jax.tree.map(lambda a: lax.all_gather(a, axis), part)  92.9 us
    psum x1, waiting for transfers between devices, body(): lax.psum(jnp.dot(normed_out, proj_head, preferred_element_type=jnp.float3...  43.5 us
    all_gather x1, waiting for transfers between devices, body(): lax.all_gather(table_head, 'ctx', axis=0, tiled=True)  42.6 us
    unnamed x7, waiting for transfers between devices  36.5 us
    all_gather x1, waiting for transfers between devices, body(): lax.all_gather(scale_rows(own_rows, own_sq, gain_in), 'tp', axis=1, tiled...  28.5 us
    all_gather x1, waiting for transfers between devices, body(): lax.all_gather(table_middle, 'ctx', axis=0, tiled=True)  22.5 us
    psum x1, blocking collectives, body(): own_sq = lax.psum(jnp.sum(own_rows * own_rows, 1), 'tp')  15 us
    psum x1, blocking collectives, body(): out_sq = lax.psum(jnp.sum(summed * summed, 1), 'tp')  14.5 us
  transfers between devices with their start and end apart: 7, of which 7 were waited for; matrix products, arithmetic and copies ran while one was open for 7% of the time, Pallas kernels for 0%

commit v1 on v0

--- a/solution.py
+++ b/solution.py
@@ -1,3 +1,4 @@
+import functools
 import jax
 import jax.numpy as jnp
 from jax import lax
@@ -8,6 +9,21 @@
 V0 = 10240
 V1 = 20480
 NEG_FILL = -1e30
+
+
+def get_gates_for(raw, dim_at):
+    return jnp.concatenate(
+        jax.lax.all_to_all(
+            jnp.stack([raw] * jax.lax.axis_size("ctx")),
+            concat_axis=0,
+            axis_name="ctx",
+            split_axis=0,
+        ),
+        axis=dim_at,
+    )
+
+
+_divide_runs = functools.partial(get_gates_for, dim_at=0)
 
 
 def passed_along(block, axis, distance):
@@ -170,10 +186,7 @@
     middle_base = tp_rank * rows_middle * ctx_count
     tail_base = tp_rank * rows_tail * ctx_count
     middle_stats = fold_band(
-        empty_stats(seg_len),
-        lax.all_gather(table_middle, "ctx", axis=0, tiled=True),
-        inputs_middle,
-        targets - V0 - middle_base,
+        empty_stats(seg_len), _divide_runs(table_middle), inputs_middle, targets - V0 - middle_base
     )
     tail_stats = fold_band(
         empty_stats(seg_len),

time: 372 us -> 322 us (0.87)
  waiting for transfers between devices: 180 us -> 124 us
  starting transfers between devices: 3.56 us -> 13.8 us
  blocking collectives: 122 us -> 116 us
    all_gather x1, waiting for transfers between devices: 42.6 us -> 0.03 us  [body(): lax.all_gather(table_head, 'ctx', axis=0, tiled=True)]
    all_gather x1, waiting for transfers between devices: 2.69 us -> 25.7 us  [body(): lax.all_gather(table_tail, 'ctx', axis=0, tiled=True)]
    all_gather x1 -> x0, waiting for transfers between devices: 22.5 us -> none  [body(): lax.all_gather(table_middle, 'ctx', axis=0, tiled=True)]
    psum x1, waiting for transfers between devices: 43.5 us -> 30.1 us  [body(): lax.psum(jnp.dot(normed_out, proj_head, preferred_element_type=jnp.float3...]
    all_to_all x0 -> x1, starting transfers between devices: none -> 10.3 us  [get_gates_for(): jax.lax.all_to_all(jnp.stack([raw] * jax.lax.axis_size('ctx')), concat_ax...]
    all_gather x9, blocking collectives: 92.9 us -> 86.6 us  [merged(): gathered = jax.tree.map(lambda a: lax.all_gather(a, axis), part)]
    unnamed x7 -> x6, waiting for transfers between devices: 36.5 us -> 36 us
  transfers between devices with their start and end apart: 7 -> 7, of which waited for: 7 -> 5; matrix products, arithmetic and copies ran while one was open for 7% -> 8% of each run, Pallas kernels for 0% -> 0%
where the time goes in v1:
time: 322 us; the launch traced here: 321 us
  waiting for transfers between devices  124 us (39%)
  blocking collectives  116 us (36%)
  matrix products  29.7 us (9%)
  between operations  15.6 us (5%)
  starting transfers between devices  13.8 us (4%)
  other arithmetic  11.4 us (4%)
  local copies, waits for them, and re-layouts  9.81 us (3%)
    all_gather x9, blocking collectives, merged(): gathered = jax.tree.map(lambda a: lax.all_gather(a, axis), part)  86.6 us
    unnamed x6, waiting for transfers between devices  36 us
    psum x1, waiting for transfers between devices, body(): lax.psum(jnp.dot(normed_out, proj_head, preferred_element_type=jnp.float3...  30.1 us
    all_gather x1, waiting for transfers between devices, body(): lax.all_gather(scale_rows(own_rows, own_sq, gain_in), 'tp', axis=1, tiled...  28.5 us
    all_gather x1, waiting for transfers between devices, body(): lax.all_gather(table_tail, 'ctx', axis=0, tiled=True)  25.7 us
    psum x1, blocking collectives, body(): own_sq = lax.psum(jnp.sum(own_rows * own_rows, 1), 'tp')  15 us
    psum x1, blocking collectives, body(): out_sq = lax.psum(jnp.sum(summed * summed, 1), 'tp')  14.5 us
    dot_general x10, matrix products, fold_band(): lax.dot_general(table_slab, band_rows, (((1,), (1,)), ((), ())), preferre...  13.7 us
  transfers between devices with their start and end apart: 7, of which 5 were waited for; matrix products, arithmetic and copies ran while one was open for 8% of the time, Pallas kernels for 0%

profile of v1, /device:TPU:1, one launch (start us, length us, event | category | flops | bytes accessed | tf_op | source)
XLA Modules:
  0.0 321.2 jit_solution(7770222255903603815)
XLA Ops:
  8.1 1.2 fusion.52
  9.3 15.0 %psum.35 = f32[256]{0:T(256)S(1)} all-reduce(f32[256]{0:T(256)S(1)} %fusion.52), channel_id=1, replica_groups=mesh['ctx'=32,'tp'=8] {'tp'}, use_global_device_ids=true, to_apply=%region_1.0 | all-reduce | flops 256 | bytes 2048 | tf_op jit(solution)/shard_map/psum | solution.py:122
  24.2 0.8 dynamic_slice.124
  25.0 1.7 fusion.54
  26.8 0.0 reduce-scatter.4.cloned.1.call-start
  26.8 28.5 %all-gather.16.cloned.1.call-done = bf16[256,3072]{1,0:T(8,128)(2,1)} async-done(((bf16[256,384]{1,0:T(8,128)(2,1)}), bf16[256,3072]{1,0:T(8,128)(2,1)}) %all-gather.16.cloned.1.call-update) | async-done | bytes 1572880 | tf_op jit(solution)/shard_map/all_gather | solution.py:123
  55.4 3.3 %convolution_convert_fusion.4 = bf16[256,384]{1,0:T(8,128)(2,1)S(1)} fusion(bf16[256,3072]{1,0:T(8,128)(2,1)} %all-gather.16.cloned.1.call-done, bf16[3072,384]{1,0:T(8,128)(2,1)} %param.21), kind=kOutput, calls=%fused_computation.66 | convolution fusion | flops 604078080 | bytes 4128768 | tf_op jit(solution)/shard_map/dot_general | solution.py:94
  58.7 1.0 convolution_convert_fusion.5
  59.7 3.3 %collective-permute-start = (bf16[256,768]{1,0:T(8,128)(2,1)S(1)}, bf16[256,768]{1,0:T(8,128)(2,1)S(1)}, u32[]{:S(2)}, u32[]{:S(2)}) collective-permute-start(bf16[256,768]{1,0:T(8,128)(2,1)S(1)} %pad_maximum_fusion), channel_id=1, source_target_pairs={{0,8},{8,16},{16,24},{24,32},{32,40},{40,48},{48,56},{56,64},{64,7... | collective-permute-start | bytes 1179656 | tf_op jit(solution)/shard_map/ppermute | solution.py:32
  63.0 0.7 fusion.51
  63.7 1.7 convolution_convert_fusion.3
  65.4 1.7 copy.24
  67.1 4.0 %collective-permute-done = bf16[256,768]{1,0:T(8,128)(2,1)S(1)} collective-permute-done((bf16[256,768]{1,0:T(8,128)(2,1)S(1)}, bf16[256,768]{1,0:T(8,128)(2,1)S(1)}, u32[]{:S(2)}, u32[]{:S(2)}) %collective-permute-start) | collective-permute-done | bytes 393248 | tf_op jit(solution)/shard_map/ppermute | solution.py:32
  71.2 0.1 pad_maximum_fusion.1
  71.3 0.2 copy.23
  71.5 0.2 copy.25
  71.7 2.0 fusion.69
  73.7 2.0 convolution_convert_fusion.6
  75.8 2.2 convolution_convert_fusion
  77.9 2.6 copy.26
  80.6 0.0 all-gather.20.cloned.1.call-start
  80.6 0.5 all-gather.20.cloned.1.call-update
  81.2 0.8 dynamic_slice.125
  82.0 34.9 %reduce-scatter.4.cloned.1.call-done = bf16[384,256]{1,0:T(8,128)(2,1)} async-done(((bf16[3072,256]{1,0:T(8,128)(2,1)}), bf16[384,256]{1,0:T(8,128)(2,1)}) %reduce-scatter.4.cloned.1.call-update) | async-done | bytes 196624
  116.9 1.1 copy.27
  118.0 0.1 multiply_reduce_fusion
  118.1 14.5 %psum.36 = f32[256]{0:T(256)S(1)} all-reduce(f32[256]{0:T(256)S(1)} %multiply_reduce_fusion), channel_id=1, replica_groups=mesh['ctx'=32,'tp'=8] {'tp'}, use_global_device_ids=true, to_apply=%region_6.7 | all-reduce | flops 256 | bytes 2048 | tf_op jit(solution)/shard_map/psum | solution.py:155
  132.6 0.7 multiply_convert_fusion
  133.4 0.8 convolution_convert_fusion.7
  134.2 1.0 convolution_convert_fusion.2
  135.2 1.7 convolution_convert_fusion.1
  136.9 0.0 all-gather.18.cloned.1.call-start
  137.0 0.5 all-gather.18.cloned.1.call-update
  137.5 1.9 stack.2
  139.4 10.3 %all-to-all-start = ((bf16[32,80,512]{2,1,0:T(8,128)(2,1)}), bf16[32,80,512]{2,1,0:T(8,128)(2,1)}, u32[]{:S(2)}, u32[]{:S(2)}) async-start(bf16[32,80,512]{2,1,0:T(8,128)(2,1)} %stack.2), calls=%async_computation | async-start | bytes 5242880 | tf_op jit(solution)/shard_map/all_to_all | solution.py:16
  149.8 25.7 %all-gather.20.cloned.1.call-done = bf16[13056,128]{1,0:T(8,128)(2,1)} async-done(((bf16[408,128]{1,0:T(8,128)(2,1)}), bf16[13056,128]{1,0:T(8,128)(2,1)}) %all-gather.20.cloned.1.call-update) | async-done | bytes 3342352 | tf_op jit(solution)/shard_map/all_gather | solution.py:193
  175.6 30.1 %all-reduce.3.cloned.1.call-done = (bf16[256,2048]{1,0:T(8,128)(2,1)}, bf16[256,512]{1,0:T(8,128)(2,1)}, bf16[256,128]{1,0:T(8,128)(2,1)}) async-done(((bf16[256,2048]{1,0:T(8,128)(2,1)}, bf16[256,512]{1,0:T(8,128)(2,1)}, bf16[256,128]{1,0:T(8,128)(2,1)}), (bf16[256,2048]{1,0:T(8,128)(2,1)}, bf16[256,512]{1,0:T(8,128)(2,1)}, bf16[256,128]{1,0:T(8,128)(2,1)})) %all-reduce.3.cloned.1.call-update) | async-done | bytes 1376272 | tf_op jit(solution)/shard_map/psum | solution.py:158
  205.6 1.4 fusion.73
  207.1 0.4 fusion.33
  207.4 1.6 fusion.78
  209.1 0.5 fusion.77
  209.6 0.5 fusion.76
  210.1 0.5 fusion.75
  210.6 0.5 fusion.74
  211.1 0.5 fusion.79
  211.7 3.4 %fusion.17 = (f32[256]{0:T(256)S(1)}, f32[256]{0:T(256)S(1)}, f32[256]{0:T(256)S(1)}, f32[256]{0:T(256)S(1)}, f32[256]{0:T(256)S(1)}, /*index=5*/f32[256]{0:T(25...) fusion(f32[256,2048]{1,0:T(8,128)S(1)} %get-tuple-element.568, ...), kind=kLoop, calls=%fused_computation.41 | loop fusion | flops 15725568 | bytes 12643328 | tf_op jit(solution)/shard_map/reduce_sum | solution.py:82
  215.1 10.6 %all-gather.10 = f32[8,1,256]{2,1,0:T(1,128)S(1)} all-gather(f32[1,1,256]{2,1,0:T(1,128)S(1)} %get-tuple-element.548), channel_id=1, replica_groups=mesh['ctx'=32,'tp'=8] {'tp'}, dimensions={0}, use_global_device_ids=true | all-gather | bytes 9216 | tf_op jit(solution)/shard_map/all_gather | solution.py:36
  225.7 9.4 %all-gather.11 = f32[8,1,256]{2,1,0:T(1,128)S(1)} all-gather(f32[1,1,256]{2,1,0:T(1,128)S(1)} %bitcast.288), channel_id=4, replica_groups=mesh['ctx'=32,'tp'=8] {'tp'}, dimensions={0}, use_global_device_ids=true | all-gather | bytes 9216 | tf_op jit(solution)/shard_map/all_gather | solution.py:36
  235.1 8.2 %all-gather.9 = f32[8,1,256]{2,1,0:T(1,128)S(1)} all-gather(f32[1,1,256]{2,1,0:T(1,128)S(1)} %get-tuple-element.549), channel_id=1, replica_groups=mesh['ctx'=32,'tp'=8] {'tp'}, dimensions={0}, use_global_device_ids=true | all-gather | bytes 9216 | tf_op jit(solution)/shard_map/all_gather | solution.py:36
  243.4 1.5 fusion.71
  244.9 0.3 fusion.50
  245.2 2.4 fusion.72
  247.7 0.8 fusion.23
  248.4 9.5 %all-gather.7 = f32[8,1,256]{2,1,0:T(1,128)S(1)} all-gather(f32[1,1,256]{2,1,0:T(1,128)S(1)} %get-tuple-element.552), channel_id=1, replica_groups=mesh['ctx'=32,'tp'=8] {'tp'}, dimensions={0}, use_global_device_ids=true | all-gather | bytes 9216 | tf_op jit(solution)/shard_map/all_gather | solution.py:36
  257.9 8.2 %all-gather.8 = f32[8,1,256]{2,1,0:T(1,128)S(1)} all-gather(f32[1,1,256]{2,1,0:T(1,128)S(1)} %bitcast.287), channel_id=3, replica_groups=mesh['ctx'=32,'tp'=8] {'tp'}, dimensions={0}, use_global_device_ids=true | all-gather | bytes 9216 | tf_op jit(solution)/shard_map/all_gather | solution.py:36
  266.1 9.5 %all-gather.6 = f32[8,1,256]{2,1,0:T(1,128)S(1)} all-gather(f32[1,1,256]{2,1,0:T(1,128)S(1)} %get-tuple-element.553), channel_id=1, replica_groups=mesh['ctx'=32,'tp'=8] {'tp'}, dimensions={0}, use_global_device_ids=true | all-gather | bytes 9216 | tf_op jit(solution)/shard_map/all_gather | solution.py:36
  275.6 0.4 fusion.80
  276.0 4.1 %fusion.70 = (f32[256]{0:T(256)S(1)}, f32[256,1280]{1,0:T(8,128)S(1)}) fusion(bf16[256,2048]{1,0:T(8,128)(2,1)S(1)} %copy-done.5, bf16[1280,2048]{1,0:T(8,128)(2,1)} %all-gather.18.cloned.1.call-done), kind=kOutput, calls=%fused_computation.154 | convolution fusion | flops 1342504704 | bytes 7603200 | tf_op jit(solution)/shard_map/dot_general | solution.py:76
  280.1 0.5 fusion.27
  280.7 13.7 %all-gather.4 = f32[8,1,256]{2,1,0:T(1,128)S(1)} all-gather(f32[1,1,256]{2,1,0:T(1,128)S(1)} %get-tuple-element.557), channel_id=1, replica_groups=mesh['ctx'=32,'tp'=8] {'tp'}, dimensions={0}, use_global_device_ids=true | all-gather | bytes 9216 | tf_op jit(solution)/shard_map/all_gather | solution.py:36
  294.4 8.1 %all-gather.5 = f32[8,1,256]{2,1,0:T(1,128)S(1)} all-gather(f32[1,1,256]{2,1,0:T(1,128)S(1)} %bitcast.282), channel_id=2, replica_groups=mesh['ctx'=32,'tp'=8] {'tp'}, dimensions={0}, use_global_device_ids=true | all-gather | bytes 9216 | tf_op jit(solution)/shard_map/all_gather | solution.py:36
  302.5 9.5 %all-gather.3 = f32[8,1,256]{2,1,0:T(1,128)S(1)} all-gather(f32[1,1,256]{2,1,0:T(1,128)S(1)} %get-tuple-element.558), channel_id=1, replica_groups=mesh['ctx'=32,'tp'=8] {'tp'}, dimensions={0}, use_global_device_ids=true | all-gather | bytes 9216 | tf_op jit(solution)/shard_map/all_gather | solution.py:36
  312.0 1.4 while.31
  313.5 0.6 compare_select_fusion.1
  (161 shorter events, 1.5 us)
Async XLA Ops:
  8.0 67.8 %copy-start = (bf16[384,3072]{1,0:T(8,128)(2,1)S(1)}, bf16[384,3072]{1,0:T(8,128)(2,1)}, u32[]{:S(2)}) copy-start(bf16[384,3072]{1,0:T(8,128)(2,1)} %param.22) | copy-start | bytes 7077892
  8.0 47.3 %all-gather.16.cloned.1.call-start = ((), (), s32[]{:S(2)}) async-start(), calls=%async_computation.2 | async-start | bytes 1769472 | tf_op jit(solution)/shard_map/all_gather | solution.py:123
  26.8 90.1 %reduce-scatter.4.cloned.1.call-start = ((), (), s32[]{:S(2)}) async-start(), calls=%async_computation.5 | async-start | bytes 1769472
  55.4 3.3 %copy-start.16 = (bf16[3072,384]{1,0:T(8,128)(2,1)S(1)}, bf16[3072,384]{1,0:T(8,128)(2,1)}, u32[]{:S(2)}) copy-start(bf16[3072,384]{1,0:T(8,128)(2,1)} %param.20) | copy-start | bytes 7077892
  55.4 3.3 %copy-start.18 = (bf16[256,3072]{1,0:T(8,128)(2,1)S(1)}, bf16[256,3072]{1,0:T(8,128)(2,1)}, u32[]{:S(2)}) copy-start(bf16[256,3072]{1,0:T(8,128)(2,1)} %all-gather.16.cloned.1.call-done) | copy-start | bytes 4718596
  58.7 5.1 %copy-start.17 = (bf16[3072,384]{1,0:T(8,128)(2,1)S(1)}, bf16[3072,384]{1,0:T(8,128)(2,1)}, u32[]{:S(2)}) copy-start(bf16[3072,384]{1,0:T(8,128)(2,1)} %param.19) | copy-start | bytes 7077892
  59.7 11.5 %collective-permute-start = (bf16[256,768]{1,0:T(8,128)(2,1)S(1)}, bf16[256,768]{1,0:T(8,128)(2,1)S(1)}, u32[]{:S(2)}, u32[]{:S(2)}) collective-permute-start(bf16[256,768]{1,0:T(8,128)(2,1)S(1)} %pad_maximum_fusion), channel_id=1, source_target_pairs={{0,8},{8,16},{16,24},{24,32},{32,40},{40,48},{48,56},{56,64},{64,7... | collective-permute-start | bytes 1179656 | tf_op jit(solution)/shard_map/ppermute | solution.py:32
  71.7 2.0 copy-start.8
  77.9 40.0 %copy-start.3 = (bf16[256,384]{1,0:T(8,128)(2,1)S(1)}, bf16[256,384]{1,0:T(8,128)(2,1)}, u32[]{:S(2)}) copy-start(bf16[256,384]{1,0:T(8,128)(2,1)} %param.17) | copy-start | bytes 589828
  80.5 52.8 %copy-start.9 = (bf16[384,128]{1,0:T(8,128)(2,1)S(1)}, bf16[384,128]{1,0:T(8,128)(2,1)}, u32[]{:S(2)}) copy-start(bf16[384,128]{1,0:T(8,128)(2,1)} %param.26) | copy-start | bytes 294916
  80.5 53.6 %copy-start.7 = (bf16[384,512]{1,0:T(8,128)(2,1)S(1)}, bf16[384,512]{1,0:T(8,128)(2,1)}, u32[]{:S(2)}) copy-start(bf16[384,512]{1,0:T(8,128)(2,1)} %param.25) | copy-start | bytes 1179652
  80.6 95.0 %all-gather.20.cloned.1.call-start = ((), (), s32[]{:S(2)}) async-start(), calls=%async_computation.4 | async-start | bytes 3446784 | tf_op jit(solution)/shard_map/all_gather | solution.py:193
  81.2 124.5 %all-reduce.3.cloned.1.call-start = ((), (), s32[]{:S(2)}) async-start(), calls=%async_computation.6 | async-start | bytes 2752512 | tf_op jit(solution)/shard_map/psum | solution.py:158
  132.6 2.6 copy-start.4
  135.2 2.3 copy-start.10
  136.9 139.1 %all-gather.18.cloned.1.call-start = ((), (), s32[]{:S(2)}) async-start(), calls=%async_computation.3 | async-start | bytes 5406720 | tf_op jit(solution)/shard_map/all_gather | solution.py:182
  139.4 10.4 %copy-start.15 = (s32[256]{0:T(256)S(1)}, s32[256]{0:T(256)}, u32[]{:S(2)}) copy-start(s32[256]{0:T(256)} %param.31) | copy-start | bytes 3076
  139.4 103.9 %all-to-all-start = ((bf16[32,80,512]{2,1,0:T(8,128)(2,1)}), bf16[32,80,512]{2,1,0:T(8,128)(2,1)}, u32[]{:S(2)}, u32[]{:S(2)}) async-start(bf16[32,80,512]{2,1,0:T(8,128)(2,1)} %stack.2), calls=%async_computation | async-start | bytes 5242880 | tf_op jit(solution)/shard_map/all_to_all | solution.py:16
  205.6 3.4 %copy-start.1 = (bf16[13056,128]{1,0:T(8,128)(2,1)S(1)}, bf16[13056,128]{1,0:T(8,128)(2,1)}, u32[]{:S(2)}) copy-start(bf16[13056,128]{1,0:T(8,128)(2,1)} %all-gather.20.cloned.1.call-done) | copy-start | bytes 10027012
  205.6 3.4 %copy-start.2 = (bf16[256,128]{1,0:T(8,128)(2,1)S(1)}, bf16[256,128]{1,0:T(8,128)(2,1)}, u32[]{:S(2)}) copy-start(bf16[256,128]{1,0:T(8,128)(2,1)} %get-tuple-element.529) | copy-start | bytes 196612
  211.7 31.7 %copy-start.6 = (bf16[256,512]{1,0:T(8,128)(2,1)S(1)}, bf16[256,512]{1,0:T(8,128)(2,1)}, u32[]{:S(2)}) copy-start(bf16[256,512]{1,0:T(8,128)(2,1)} %get-tuple-element.528) | copy-start | bytes 786436
  225.7 21.9 %copy-start.12 = (f32[8,1,256]{2,1,0:T(1,128)}, f32[8,1,256]{2,1,0:T(1,128)S(1)}, u32[]{:S(2)}) copy-start(f32[8,1,256]{2,1,0:T(1,128)S(1)} %all-gather.10) | copy-start | bytes 24580
  235.1 12.5 %copy-start.11 = (f32[8,1,256]{2,1,0:T(1,128)}, f32[8,1,256]{2,1,0:T(1,128)S(1)}, u32[]{:S(2)}) copy-start(f32[8,1,256]{2,1,0:T(1,128)S(1)} %all-gather.11) | copy-start | bytes 24580
  243.4 4.3 %copy-start.13 = (f32[8,1,256]{2,1,0:T(1,128)}, f32[8,1,256]{2,1,0:T(1,128)S(1)}, u32[]{:S(2)}) copy-start(f32[8,1,256]{2,1,0:T(1,128)S(1)} %all-gather.9) | copy-start | bytes 24580
  247.6 27.9 %copy-start.5 = (bf16[256,2048]{1,0:T(8,128)(2,1)S(1)}, bf16[256,2048]{1,0:T(8,128)(2,1)}, u32[]{:S(2)}) copy-start(bf16[256,2048]{1,0:T(8,128)(2,1)} %get-tuple-element.527) | copy-start | bytes 3145732
  247.6 27.9 %copy-start.14 = (bf16[2,2048]{1,0:T(2,128)(2,1)S(1)}, bf16[2,2048]{1,0:T(2,128)(2,1)}, u32[]{:S(2)}) copy-start(bf16[2,2048]{1,0:T(2,128)(2,1)} %param.30) | copy-start | bytes 24580
  275.9 36.1 %slice-start = ((f32[8,1,256]{2,1,0:T(1,128)}), f32[1,1,256]{2,1,0:T(1,128)S(1)}, s32[]{:S(2)}) async-start(f32[8,1,256]{2,1,0:T(1,128)} %copy-done.11), calls=%async_computation.7 | async-start | bytes 2048 | tf_op jit(solution)/shard_map/jit(dynamic_index_in_dim)/dynamic_slice | solution.py:39
  275.9 36.1 %slice-start.1 = ((f32[8,1,256]{2,1,0:T(1,128)}), f32[1,1,256]{2,1,0:T(1,128)S(1)}, s32[]{:S(2)}) async-start(f32[8,1,256]{2,1,0:T(1,128)} %copy-done.12), calls=%async_computation.8 | async-start | bytes 2048 | tf_op jit(solution)/shard_map/jit(dynamic_index_in_dim)/dynamic_slice | solution.py:39
  276.0 36.1 %slice-start.2 = ((f32[8,1,256]{2,1,0:T(1,128)}), f32[1,1,256]{2,1,0:T(1,128)S(1)}, s32[]{:S(2)}) async-start(f32[8,1,256]{2,1,0:T(1,128)} %copy-done.13), calls=%async_computation.9 | async-start | bytes 2048 | tf_op jit(solution)/shard_map/jit(dynamic_index_in_dim)/dynamic_slice | solution.py:39
Sparse Core Ops, SparseCore 0:
  26.9 28.4 all-gather.15
  80.7 36.1 reduce-scatter.3
  137.1 68.5 all-reduce.2
Sparse Core Ops, SparseCore 1:
  83.6 91.9 all-gather.19
  178.0 97.5 all-gather.17
